TPU v7x, 32 devices: a whole 2x2x4 slice. The times are simulated.
32 devices in a mesh: rows: 8 (over z, y), dims: 4 (over x, core).
Axes of the slice: x: 2, y: 2, z: 4, core: 2. Of those that a mesh axis runs over, the one named last changes fastest.
Arguments:
- table: bfloat16 [1, 256, 32768], P(None, 'dims', 'rows'), may hold values from -6 to 6
- accum: float32 [1, 32768], P(None, 'rows'), may hold values from 0.5 to 8
- grad_pooled: bfloat16 [1, 256, 1024], P(None, 'dims', 'rows'), may hold values from -6 to 6
- sample_slot: int32 [1, 8, 8, 1280], P(None, 'rows'), may hold values from 0 to 127
- row_slot: int32 [1, 8, 8, 1280], P(None, 'rows'), may hold values from 0 to 4095
- weight: int32 [1, 8, 8, 1280], P(None, 'rows'), may hold values from 1 to 3
- send_count: int32 [1, 8, 8], P(None, 'rows'), may hold values from 1 to 1280, as said below
Outputs:
- pooled: float32 [1, 256, 1024], P(None, 'dims', 'rows')
- new_table: bfloat16 [1, 256, 32768], P(None, 'dims', 'rows')
- new_accum: float32 [1, 32768], P(None, 'rows')
Inputs may be any that keep to these rules, and one draw needn't show every extreme that they name: `send_count`: at most 1280 live entries from one row shard to one owner per feature; in every feature one owner receives exactly 1280 from every row shard. Slots at or after the count are unused.
All inputs are finite; a program needn't handle non-finite values.
Results may differ from a plain program's by a relative error of at most 0.001.
Values may be sent and summed in bfloat16 or wider, within the bound.
No kernel may reach another device: no remote copies, remote signals or barrier semaphores. Data moves between devices by JAX's collectives and lax.ppermute only.
A program may use at most 64 MiB of HBM per device.

v0:
```python
import math
import jax
import jax.numpy as jnp
from jax import lax
from jax.sharding import PartitionSpec as P

D = 256
step_size = 0.3


def shards(table, accum, grad_pooled, sample_slot, row_slot, weight, send_count):
    feat_count, dim_local, row_local = table.shape
    peer_count = lax.axis_size("rows")
    own_samples = grad_pooled.shape[2]
    slot_count = sample_slot.shape[3]
    entry_count = peer_count * slot_count
    block_rows = math.gcd(row_local, 512)
    block_count = row_local // block_rows
    sample_local = sample_slot.reshape(feat_count, peer_count, slot_count)
    row_index = row_slot.reshape(feat_count, peer_count, slot_count)
    flat_rows = row_index.reshape(feat_count, 1, entry_count)
    live_count = send_count.reshape(feat_count, peer_count)
    slot_iota = lax.broadcasted_iota(jnp.int32, (1, 1, slot_count), 2)
    live_mask = slot_iota < live_count[:, :, None]
    weights = jnp.where(live_mask, weight.reshape(feat_count, peer_count, slot_count), 0)
    flat_weights = weights.reshape(feat_count, 1, entry_count).astype(jnp.bfloat16)
    block_iota = lax.broadcasted_iota(jnp.int32, (1, block_rows, 1), 1)

    def lookup_block(carry, block):
        start = block * block_rows
        table_part = lax.dynamic_slice_in_dim(table, start, block_rows, 2)
        selector = (flat_rows == block_iota + start).astype(jnp.bfloat16)
        return (
            carry
            + jnp.einsum("fdr,fre->fde", table_part, selector, preferred_element_type=jnp.float32),
            None,
        )

    looked_up, _ = lax.scan(
        lookup_block,
        jnp.zeros((feat_count, dim_local, entry_count), jnp.float32),
        jnp.arange(block_count, dtype=jnp.int32),
    )
    picked = looked_up.astype(jnp.bfloat16).reshape(feat_count, dim_local, peer_count, slot_count)
    positions = lax.broadcasted_iota(jnp.int32, (1, 1, 1, own_samples), 3)
    onehot = jnp.where(sample_local[..., None] == positions, weights[..., None], 0).astype(
        jnp.bfloat16
    )
    pooled = lax.psum_scatter(
        jnp.einsum("fdnk,fnkj->nfdj", picked, onehot, preferred_element_type=jnp.float32),
        "rows",
        scatter_dimension=0,
        tiled=True,
    ).reshape(feat_count, dim_local, own_samples)
    all_grads = lax.all_gather(grad_pooled, "rows", axis=2, tiled=True)
    all_grads = all_grads.reshape(feat_count, dim_local, peer_count, own_samples)
    selector = (sample_local[..., None] == positions).astype(jnp.bfloat16)
    entry_values = jnp.einsum(
        "fdnj,fnkj->fdnk", all_grads, selector, preferred_element_type=jnp.float32
    ).astype(jnp.bfloat16)
    entry_flat = entry_values.reshape(feat_count, dim_local, entry_count)

    def gradient_block(block):
        start = block * block_rows
        weighted = jnp.where(flat_rows == block_iota + start, flat_weights, 0)
        return jnp.einsum("fde,fre->fdr", entry_flat, weighted, preferred_element_type=jnp.float32)

    grad_blocks = lax.map(gradient_block, jnp.arange(block_count, dtype=jnp.int32))
    row_grad = jnp.moveaxis(grad_blocks, 0, 2).reshape(feat_count, dim_local, row_local)
    squares = jnp.sum(row_grad * row_grad, axis=1)
    norm_total = lax.psum(squares, "dims")
    new_accum = accum + norm_total / D
    new_table = (
        table.astype(jnp.float32) - step_size * row_grad / jnp.sqrt(new_accum)[:, None, :]
    ).astype(jnp.bfloat16)
    return (pooled, new_table, new_accum)


def solution(mesh):
    return jax.shard_map(
        shards,
        mesh=mesh,
        in_specs=(
            P(None, "dims", "rows"),
            P(None, "rows"),
            P(None, "dims", "rows"),
            P(None, "rows", None, None),
            P(None, "rows", None, None),
            P(None, "rows", None, None),
            P(None, "rows", None),
        ),
        out_specs=(P(None, "dims", "rows"), P(None, "dims", "rows"), P(None, "rows")),
        check_vma=False,
    )
```

profile of v0, /device:TPU:0, one launch (start us, length us, event | category | flops | bytes accessed | tf_op | source)
XLA Modules:
  0.0 151.7 jit_solution(12816893557992294160)
XLA Ops:
  7.2 0.0 reduce-scatter.2.cloned.1.call-start
  7.2 0.8 reshape_reshape.3
  8.1 48.6 %while.25 = (s32[]{:T(128)}, f32[1,64,10240]{2,1,0:T(8,128)S(1)}, s32[8]{0:T(128)S(1)}, bf16[1,64,4096]{2,1,0:T(8,128)(2,1)}, s32[1,1,10240]{2,1,0:T(1,128)S(1)}...) while((s32[]{:T(128)}, f32[1,64,10240]{2,1,0:T(8,128)S(1)}, s32[8]{0:T(128)S(1)}, ...), condition=%wide.region_1.2_spmd.clone, body=%wide.region_0.1_spmd.clone.sunk | while | flops 677642752 | bytes 5353649 | solution.py:39
  8.1 0.6 dynamic_slice.25
  9.3 4.8 %fusion.55 = f32[1,64,10240]{2,1,0:T(8,128)S(1)} fusion(s32[10240]{0:T(1024)S(1)} %bitcast.90, s32[512]{0:T(512)S(1)} %bitcast.88, f32[1,64,10240]{2,1,0:T(8,128)S(1)} %get-tuple-element.264, pred[]{:T(512)S(6)} %compare.3, bf16[1,64,4096]{2,1,0:T(8,128)(2,1)} %get-tuple-element.275, s32[]{:T(128)S(6)} %select_n.63), kind=kOutput, calls=%fused_computation.5.clone.1 | convolution fusion | flops 677642240 | bytes 5351429 | tf_op jit(solution)/shard_map/while/body/eval_jaxpr/fdr,fre->fde/dot_general | solution.py:35
  14.1 0.6 dynamic_slice.25
  15.4 4.8 %fusion.55 = f32[1,64,10240]{2,1,0:T(8,128)S(1)} fusion(s32[10240]{0:T(1024)S(1)} %bitcast.90, s32[512]{0:T(512)S(1)} %bitcast.88, f32[1,64,10240]{2,1,0:T(8,128)S(1)} %get-tuple-element.264, pred[]{:T(512)S(6)} %compare.3, bf16[1,64,4096]{2,1,0:T(8,128)(2,1)} %get-tuple-element.275, s32[]{:T(128)S(6)} %select_n.63), kind=kOutput, calls=%fused_computation.5.clone.1 | convolution fusion | flops 677642240 | bytes 5351429 | tf_op jit(solution)/shard_map/while/body/eval_jaxpr/fdr,fre->fde/dot_general | solution.py:35
  20.2 0.6 dynamic_slice.25
  21.5 4.8 %fusion.55 = f32[1,64,10240]{2,1,0:T(8,128)S(1)} fusion(s32[10240]{0:T(1024)S(1)} %bitcast.90, s32[512]{0:T(512)S(1)} %bitcast.88, f32[1,64,10240]{2,1,0:T(8,128)S(1)} %get-tuple-element.264, pred[]{:T(512)S(6)} %compare.3, bf16[1,64,4096]{2,1,0:T(8,128)(2,1)} %get-tuple-element.275, s32[]{:T(128)S(6)} %select_n.63), kind=kOutput, calls=%fused_computation.5.clone.1 | convolution fusion | flops 677642240 | bytes 5351429 | tf_op jit(solution)/shard_map/while/body/eval_jaxpr/fdr,fre->fde/dot_general | solution.py:35
  26.3 0.6 dynamic_slice.25
  27.5 4.8 %fusion.55 = f32[1,64,10240]{2,1,0:T(8,128)S(1)} fusion(s32[10240]{0:T(1024)S(1)} %bitcast.90, s32[512]{0:T(512)S(1)} %bitcast.88, f32[1,64,10240]{2,1,0:T(8,128)S(1)} %get-tuple-element.264, pred[]{:T(512)S(6)} %compare.3, bf16[1,64,4096]{2,1,0:T(8,128)(2,1)} %get-tuple-element.275, s32[]{:T(128)S(6)} %select_n.63), kind=kOutput, calls=%fused_computation.5.clone.1 | convolution fusion | flops 677642240 | bytes 5351429 | tf_op jit(solution)/shard_map/while/body/eval_jaxpr/fdr,fre->fde/dot_general | solution.py:35
  32.4 0.6 dynamic_slice.25
  33.6 4.8 %fusion.55 = f32[1,64,10240]{2,1,0:T(8,128)S(1)} fusion(s32[10240]{0:T(1024)S(1)} %bitcast.90, s32[512]{0:T(512)S(1)} %bitcast.88, f32[1,64,10240]{2,1,0:T(8,128)S(1)} %get-tuple-element.264, pred[]{:T(512)S(6)} %compare.3, bf16[1,64,4096]{2,1,0:T(8,128)(2,1)} %get-tuple-element.275, s32[]{:T(128)S(6)} %select_n.63), kind=kOutput, calls=%fused_computation.5.clone.1 | convolution fusion | flops 677642240 | bytes 5351429 | tf_op jit(solution)/shard_map/while/body/eval_jaxpr/fdr,fre->fde/dot_general | solution.py:35
  38.4 0.6 dynamic_slice.25
  39.7 4.8 %fusion.55 = f32[1,64,10240]{2,1,0:T(8,128)S(1)} fusion(s32[10240]{0:T(1024)S(1)} %bitcast.90, s32[512]{0:T(512)S(1)} %bitcast.88, f32[1,64,10240]{2,1,0:T(8,128)S(1)} %get-tuple-element.264, pred[]{:T(512)S(6)} %compare.3, bf16[1,64,4096]{2,1,0:T(8,128)(2,1)} %get-tuple-element.275, s32[]{:T(128)S(6)} %select_n.63), kind=kOutput, calls=%fused_computation.5.clone.1 | convolution fusion | flops 677642240 | bytes 5351429 | tf_op jit(solution)/shard_map/while/body/eval_jaxpr/fdr,fre->fde/dot_general | solution.py:35
  44.5 0.6 dynamic_slice.25
  45.8 4.8 %fusion.55 = f32[1,64,10240]{2,1,0:T(8,128)S(1)} fusion(s32[10240]{0:T(1024)S(1)} %bitcast.90, s32[512]{0:T(512)S(1)} %bitcast.88, f32[1,64,10240]{2,1,0:T(8,128)S(1)} %get-tuple-element.264, pred[]{:T(512)S(6)} %compare.3, bf16[1,64,4096]{2,1,0:T(8,128)(2,1)} %get-tuple-element.275, s32[]{:T(128)S(6)} %select_n.63), kind=kOutput, calls=%fused_computation.5.clone.1 | convolution fusion | flops 677642240 | bytes 5351429 | tf_op jit(solution)/shard_map/while/body/eval_jaxpr/fdr,fre->fde/dot_general | solution.py:35
  50.6 0.6 dynamic_slice.25
  51.8 4.8 %fusion.55 = f32[1,64,10240]{2,1,0:T(8,128)S(1)} fusion(s32[10240]{0:T(1024)S(1)} %bitcast.90, s32[512]{0:T(512)S(1)} %bitcast.88, f32[1,64,10240]{2,1,0:T(8,128)S(1)} %get-tuple-element.264, pred[]{:T(512)S(6)} %compare.3, bf16[1,64,4096]{2,1,0:T(8,128)(2,1)} %get-tuple-element.275, s32[]{:T(128)S(6)} %select_n.63), kind=kOutput, calls=%fused_computation.5.clone.1 | convolution fusion | flops 677642240 | bytes 5351429 | tf_op jit(solution)/shard_map/while/body/eval_jaxpr/fdr,fre->fde/dot_general | solution.py:35
  56.6 0.0 copy-start.1
  56.6 0.0 copy-start.4
  56.7 0.0 copy-start.5
  56.7 0.1 convert_element_type.41
  56.8 0.2 copy.18
  57.0 0.4 copy-done.1
  57.4 0.1 bitcast_select_fusion
  57.5 5.2 %fusion.39 = f32[8,1,64,128]{3,2,0,1:T(8,128)} fusion(s32[8,1280]{1,0:T(8,128)S(1)} %bitcast_select_fusion, s32[8,1280]{1,0:T(8,128)S(1)} %bitcast.94, bf16[64,8,1280]{2,1,0:T(8,128)(2,1)S(1)} %bitcast.82), kind=kOutput, calls=%fused_computation.34 | convolution fusion | flops 171704320 | bytes 1654784 | tf_op jit(solution)/shard_map/fdnk,fnkj->nfdj/dot_general | solution.py:50
  62.6 0.0 reduce-scatter.2.cloned.1.call-update
  62.8 0.1 lt.56
  62.9 28.1 %all_gather.3 = bf16[1,64,1024]{2,1,0:T(8,128)(2,1)S(1)} all-gather(bf16[1,64,128]{2,1,0:T(8,128)(2,1)S(1)} %copy-done.2), channel_id=1, replica_groups=mesh['rows'=8,'dims'=4] {'rows'}, dimensions={2}, use_global_device_ids=true | all-gather | bytes 147456 | tf_op jit(solution)/shard_map/all_gather | solution.py:55
  91.0 3.1 %fusion.32 = bf16[1,8,8,8,1280]{4,3,2,1,0:T(8,128)(2,1)S(1)} fusion(s32[8,1280]{1,0:T(8,128)S(1)} %bitcast.95, bf16[64,8,128]{2,1,0:T(8,128)(2,1)S(1)} %bitcast.84), kind=kOutput, calls=%fused_computation.27 | convolution fusion | flops 169738240 | bytes 1482752 | tf_op jit(solution)/shard_map/fdnj,fnkj->fdnk/dot_general | solution.py:58
  94.2 0.1 copy.16
  94.3 0.1 fusion.43
  94.3 38.5 %while.24 = (s32[]{:T(128)}, f32[8,1,64,512]{3,2,1,0:T(8,128)S(1)}, s32[1,1,10240]{2,1,0:T(1,128)S(1)}, s32[8]{0:T(128)S(1)}, bf16[1,1,10240]{2,1,0:T(2,128)(2,1...) while((s32[]{:T(128)}, f32[8,1,64,512]{3,2,1,0:T(8,128)S(1)}, ...), condition=%wide.region_4.5_spmd.clone, body=%wide.region_3.4_spmd.clone.sunk | while | flops 681574912 | bytes 1548423 | solution.py:68
  94.4 0.6 dynamic_slice.23
  95.6 0.1 reduce.5
  95.7 3.4 %fusion.52 = f32[8,1,64,512]{3,2,1,0:T(8,128)S(1)} fusion(f32[8,1,64,512]{3,2,1,0:T(8,128)S(1)} %get-tuple-element.291, s32[]{:T(128)S(6)} %copy.36, bf16[1,64,10240]{2,1,0:T(8,128)(2,1)S(1)} %get-tuple-element.304, s32[10240]{0:T(1024)S(1)} %bitcast.91, s32[512]{0:T(512)S(1)} %bitcast.89, bf16[10240]{0:T(1024)(128)(2,1)S(1)} %reduce.5), kind=kOutput, calls=%fused_computation.20.clone.1 | convolution fusion | flops 681574400 | bytes 1505284 | tf_op jit(solution)/shard_map/while/body/eval_jaxpr/fde,fre->fdr/dot_general | solution.py:66
  99.2 0.6 dynamic_slice.23
  100.4 0.1 reduce.5
  100.5 3.4 %fusion.52 = f32[8,1,64,512]{3,2,1,0:T(8,128)S(1)} fusion(f32[8,1,64,512]{3,2,1,0:T(8,128)S(1)} %get-tuple-element.291, s32[]{:T(128)S(6)} %copy.36, bf16[1,64,10240]{2,1,0:T(8,128)(2,1)S(1)} %get-tuple-element.304, s32[10240]{0:T(1024)S(1)} %bitcast.91, s32[512]{0:T(512)S(1)} %bitcast.89, bf16[10240]{0:T(1024)(128)(2,1)S(1)} %reduce.5), kind=kOutput, calls=%fused_computation.20.clone.1 | convolution fusion | flops 681574400 | bytes 1505284 | tf_op jit(solution)/shard_map/while/body/eval_jaxpr/fde,fre->fdr/dot_general | solution.py:66
  104.0 0.6 dynamic_slice.23
  105.2 0.1 reduce.5
  105.3 3.4 %fusion.52 = f32[8,1,64,512]{3,2,1,0:T(8,128)S(1)} fusion(f32[8,1,64,512]{3,2,1,0:T(8,128)S(1)} %get-tuple-element.291, s32[]{:T(128)S(6)} %copy.36, bf16[1,64,10240]{2,1,0:T(8,128)(2,1)S(1)} %get-tuple-element.304, s32[10240]{0:T(1024)S(1)} %bitcast.91, s32[512]{0:T(512)S(1)} %bitcast.89, bf16[10240]{0:T(1024)(128)(2,1)S(1)} %reduce.5), kind=kOutput, calls=%fused_computation.20.clone.1 | convolution fusion | flops 681574400 | bytes 1505284 | tf_op jit(solution)/shard_map/while/body/eval_jaxpr/fde,fre->fdr/dot_general | solution.py:66
  108.8 0.6 dynamic_slice.23
  110.0 0.1 reduce.5
  110.1 3.4 %fusion.52 = f32[8,1,64,512]{3,2,1,0:T(8,128)S(1)} fusion(f32[8,1,64,512]{3,2,1,0:T(8,128)S(1)} %get-tuple-element.291, s32[]{:T(128)S(6)} %copy.36, bf16[1,64,10240]{2,1,0:T(8,128)(2,1)S(1)} %get-tuple-element.304, s32[10240]{0:T(1024)S(1)} %bitcast.91, s32[512]{0:T(512)S(1)} %bitcast.89, bf16[10240]{0:T(1024)(128)(2,1)S(1)} %reduce.5), kind=kOutput, calls=%fused_computation.20.clone.1 | convolution fusion | flops 681574400 | bytes 1505284 | tf_op jit(solution)/shard_map/while/body/eval_jaxpr/fde,fre->fdr/dot_general | solution.py:66
  113.6 0.6 dynamic_slice.23
  114.8 0.1 reduce.5
  115.0 3.4 %fusion.52 = f32[8,1,64,512]{3,2,1,0:T(8,128)S(1)} fusion(f32[8,1,64,512]{3,2,1,0:T(8,128)S(1)} %get-tuple-element.291, s32[]{:T(128)S(6)} %copy.36, bf16[1,64,10240]{2,1,0:T(8,128)(2,1)S(1)} %get-tuple-element.304, s32[10240]{0:T(1024)S(1)} %bitcast.91, s32[512]{0:T(512)S(1)} %bitcast.89, bf16[10240]{0:T(1024)(128)(2,1)S(1)} %reduce.5), kind=kOutput, calls=%fused_computation.20.clone.1 | convolution fusion | flops 681574400 | bytes 1505284 | tf_op jit(solution)/shard_map/while/body/eval_jaxpr/fde,fre->fdr/dot_general | solution.py:66
  118.4 0.6 dynamic_slice.23
  119.7 0.1 reduce.5
  119.8 3.4 %fusion.52 = f32[8,1,64,512]{3,2,1,0:T(8,128)S(1)} fusion(f32[8,1,64,512]{3,2,1,0:T(8,128)S(1)} %get-tuple-element.291, s32[]{:T(128)S(6)} %copy.36, bf16[1,64,10240]{2,1,0:T(8,128)(2,1)S(1)} %get-tuple-element.304, s32[10240]{0:T(1024)S(1)} %bitcast.91, s32[512]{0:T(512)S(1)} %bitcast.89, bf16[10240]{0:T(1024)(128)(2,1)S(1)} %reduce.5), kind=kOutput, calls=%fused_computation.20.clone.1 | convolution fusion | flops 681574400 | bytes 1505284 | tf_op jit(solution)/shard_map/while/body/eval_jaxpr/fde,fre->fdr/dot_general | solution.py:66
  123.2 0.6 dynamic_slice.23
  124.5 0.1 reduce.5
  124.6 3.4 %fusion.52 = f32[8,1,64,512]{3,2,1,0:T(8,128)S(1)} fusion(f32[8,1,64,512]{3,2,1,0:T(8,128)S(1)} %get-tuple-element.291, s32[]{:T(128)S(6)} %copy.36, bf16[1,64,10240]{2,1,0:T(8,128)(2,1)S(1)} %get-tuple-element.304, s32[10240]{0:T(1024)S(1)} %bitcast.91, s32[512]{0:T(512)S(1)} %bitcast.89, bf16[10240]{0:T(1024)(128)(2,1)S(1)} %reduce.5), kind=kOutput, calls=%fused_computation.20.clone.1 | convolution fusion | flops 681574400 | bytes 1505284 | tf_op jit(solution)/shard_map/while/body/eval_jaxpr/fde,fre->fdr/dot_general | solution.py:66
  128.0 0.6 dynamic_slice.23
  129.3 0.1 reduce.5
  129.4 3.4 %fusion.52 = f32[8,1,64,512]{3,2,1,0:T(8,128)S(1)} fusion(f32[8,1,64,512]{3,2,1,0:T(8,128)S(1)} %get-tuple-element.291, s32[]{:T(128)S(6)} %copy.36, bf16[1,64,10240]{2,1,0:T(8,128)(2,1)S(1)} %get-tuple-element.304, s32[10240]{0:T(1024)S(1)} %bitcast.91, s32[512]{0:T(512)S(1)} %bitcast.89, bf16[10240]{0:T(1024)(128)(2,1)S(1)} %reduce.5), kind=kOutput, calls=%fused_computation.20.clone.1 | convolution fusion | flops 681574400 | bytes 1505284 | tf_op jit(solution)/shard_map/while/body/eval_jaxpr/fde,fre->fdr/dot_general | solution.py:66
  132.8 0.0 copy-start.3
  132.8 0.2 multiply_reduce_fusion
  133.0 0.1 copy.17
  133.1 10.1 %psum.7 = f32[1,4096]{1,0:T(1,128)S(1)} all-reduce(f32[1,4096]{1,0:T(1,128)S(1)} %bitcast.87), channel_id=1, replica_groups=mesh['rows'=8,'dims'=4] {'dims'}, use_global_device_ids=true, to_apply=%region_6.7 | all-reduce | flops 4096 | bytes 32768 | tf_op jit(solution)/shard_map/psum | solution.py:71
  143.2 0.6 fusion.45
  143.9 0.9 subtract_convert_fusion
  (34 shorter events, 0.3 us)
Async XLA Ops:
  7.2 137.7 %reduce-scatter.2.cloned.1.call-start = ((), (), s32[]{:S(2)}) async-start(), calls=%async_computation.1 | async-start | bytes 294912 | tf_op jit(solution)/shard_map/reduce_scatter | solution.py:49
  56.6 0.8 copy-start.1
  56.6 0.8 copy-start.4
  56.7 0.8 copy-start.5
  57.5 5.4 %copy-start.2 = (bf16[1,64,128]{2,1,0:T(8,128)(2,1)S(1)}, bf16[1,64,128]{2,1,0:T(8,128)(2,1)}, u32[]{:S(2)}) copy-start(bf16[1,64,128]{2,1,0:T(8,128)(2,1)} %param.13) | copy-start | bytes 49156
  132.8 10.4 %copy-start.3 = (f32[1,4096]{1,0:T(1,128)S(1)}, f32[1,4096]{1,0:T(1,128)}, u32[]{:S(2)}) copy-start(f32[1,4096]{1,0:T(1,128)} %param.12) | copy-start | bytes 49156
  132.8 11.1 %copy-start = (bf16[1,64,4096]{2,1,0:T(8,128)(2,1)S(1)}, bf16[1,64,4096]{2,1,0:T(8,128)(2,1)}, u32[]{:S(2)}) copy-start(bf16[1,64,4096]{2,1,0:T(8,128)(2,1)} %get-tuple-element.309) | copy-start | bytes 1572868
Sparse Core Ops, SparseCore 0:
  62.8 64.8 reduce-scatter.1
where the time goes:
time: 152 us
  matrix products  73.9 us (49%)
  blocking collectives  38.2 us (25%)
  between operations  14.2 us (9%)
  local copies, waits for them, and re-layouts  11.3 us (7%)
  loops' own time  11 us (7%)
  other arithmetic  3.03 us (2%)
    dot_general x8, matrix products, lookup_block(): jnp.einsum('fdr,fre->fde', table_part, selector, preferred_element_type=j...  38.3 us
    all_gather x1, blocking collectives, shards(): all_grads = lax.all_gather(grad_pooled, 'rows', axis=2, tiled=True)  28.1 us
    dot_general x8, matrix products, gradient_block(): jnp.einsum('fde,fre->fdr', entry_flat, weighted, preferred_element_type=j...  27.4 us
    psum x1, blocking collectives, shards(): norm_total = lax.psum(squares, 'dims')  10.1 us
    dynamic_slice x16, local copies, waits for them, and re-layouts, shards(): lax.scan(lookup_block, jnp.zeros((feat_count, dim_local, entry_count), jn...  9.38 us
    another operation x1, loops' own time, shards(): lax.scan(lookup_block, jnp.zeros((feat_count, dim_local, entry_count), jn...  5.55 us
    another operation x1, loops' own time, shards(): lax.map(gradient_block, jnp.arange(block_count, dtype=jnp.int32))  5.46 us
    dot_general x1, matrix products, shards(): jnp.einsum('fdnk,fnkj->nfdj', picked, onehot, preferred_element_type=jnp....  5.15 us
  transfers between devices with their start and end apart: 1, of which 0 were waited for; matrix products, arithmetic and copies ran while one was open for 25% of the time, Pallas kernels for 0%

commit v1 on v0

--- a/solution.py
+++ b/solution.py
@@ -68,7 +68,7 @@
     grad_blocks = lax.map(gradient_block, jnp.arange(block_count, dtype=jnp.int32))
     row_grad = jnp.moveaxis(grad_blocks, 0, 2).reshape(feat_count, dim_local, row_local)
     squares = jnp.sum(row_grad * row_grad, axis=1)
-    norm_total = lax.psum(squares, "dims")
+    norm_total = jnp.sum(lax.all_gather(squares, "dims"), axis=0)
     new_accum = accum + norm_total / D
     new_table = (
         table.astype(jnp.float32) - step_size * row_grad / jnp.sqrt(new_accum)[:, None, :]

time: 152 us -> 148 us (0.974)
  blocking collectives: 38.2 us -> 33.3 us
    psum x1 -> x0, blocking collectives: 10.1 us -> none  [shards(): norm_total = lax.psum(squares, 'dims')]
    all_gather x0 -> x1, blocking collectives: none -> 5.24 us  [shards(): norm_total = jnp.sum(lax.all_gather(squares, 'dims'), axis=0)]
  transfers between devices with their start and end apart: 1 -> 1, of which waited for: 0 -> 0; matrix products, arithmetic and copies ran while one was open for 25% -> 26% of each run, Pallas kernels for 0% -> 0%
where the time goes in v1:
time: 148 us; the launch traced here: 147 us
  matrix products  73.9 us (50%)
  blocking collectives  33.3 us (22%)
  between operations  14.2 us (10%)
  local copies, waits for them, and re-layouts  11.3 us (8%)
  loops' own time  11 us (7%)
  other arithmetic  3.1 us (2%)
    dot_general x8, matrix products, lookup_block(): jnp.einsum('fdr,fre->fde', table_part, selector, preferred_element_type=j...  38.3 us
    all_gather x1, blocking collectives, shards(): all_grads = lax.all_gather(grad_pooled, 'rows', axis=2, tiled=True)  28.1 us
    dot_general x8, matrix products, gradient_block(): jnp.einsum('fde,fre->fdr', entry_flat, weighted, preferred_element_type=j...  27.4 us
    dynamic_slice x16, local copies, waits for them, and re-layouts, shards(): lax.scan(lookup_block, jnp.zeros((feat_count, dim_local, entry_count), jn...  9.38 us
    another operation x1, loops' own time, shards(): lax.scan(lookup_block, jnp.zeros((feat_count, dim_local, entry_count), jn...  5.55 us
    another operation x1, loops' own time, shards(): lax.map(gradient_block, jnp.arange(block_count, dtype=jnp.int32))  5.46 us
    all_gather x1, blocking collectives, shards(): norm_total = jnp.sum(lax.all_gather(squares, 'dims'), axis=0)  5.24 us
    dot_general x1, matrix products, shards(): jnp.einsum('fdnk,fnkj->nfdj', picked, onehot, preferred_element_type=jnp....  5.15 us
  transfers between devices with their start and end apart: 1, of which 0 were waited for; matrix products, arithmetic and copies ran while one was open for 26% of the time, Pallas kernels for 0%

profile of v1, /device:TPU:0, one launch (start us, length us, event | category | flops | bytes accessed | tf_op | source)
XLA Modules:
  0.0 146.9 jit_solution(11211626491128527510)
XLA Ops:
  7.2 0.0 reduce-scatter.2.cloned.1.call-start
  7.2 0.8 reshape_reshape.3
  8.1 48.6 %while.25 = (s32[]{:T(128)}, f32[1,64,10240]{2,1,0:T(8,128)S(1)}, s32[8]{0:T(128)S(1)}, bf16[1,64,4096]{2,1,0:T(8,128)(2,1)}, s32[1,1,10240]{2,1,0:T(1,128)S(1)}...) while((s32[]{:T(128)}, f32[1,64,10240]{2,1,0:T(8,128)S(1)}, s32[8]{0:T(128)S(1)}, ...), condition=%wide.region_1.2_spmd.clone, body=%wide.region_0.1_spmd.clone.sunk | while | flops 677642752 | bytes 5353649 | solution.py:39
  8.1 0.6 dynamic_slice.25
  9.3 4.8 %fusion.55 = f32[1,64,10240]{2,1,0:T(8,128)S(1)} fusion(s32[10240]{0:T(1024)S(1)} %bitcast.87, s32[512]{0:T(512)S(1)} %bitcast.85, f32[1,64,10240]{2,1,0:T(8,128)S(1)} %get-tuple-element.264, pred[]{:T(512)S(6)} %compare.3, bf16[1,64,4096]{2,1,0:T(8,128)(2,1)} %get-tuple-element.275, s32[]{:T(128)S(6)} %select_n.63), kind=kOutput, calls=%fused_computation.5.clone.1 | convolution fusion | flops 677642240 | bytes 5351429 | tf_op jit(solution)/shard_map/while/body/eval_jaxpr/fdr,fre->fde/dot_general | solution.py:35
  14.1 0.6 dynamic_slice.25
  15.4 4.8 %fusion.55 = f32[1,64,10240]{2,1,0:T(8,128)S(1)} fusion(s32[10240]{0:T(1024)S(1)} %bitcast.87, s32[512]{0:T(512)S(1)} %bitcast.85, f32[1,64,10240]{2,1,0:T(8,128)S(1)} %get-tuple-element.264, pred[]{:T(512)S(6)} %compare.3, bf16[1,64,4096]{2,1,0:T(8,128)(2,1)} %get-tuple-element.275, s32[]{:T(128)S(6)} %select_n.63), kind=kOutput, calls=%fused_computation.5.clone.1 | convolution fusion | flops 677642240 | bytes 5351429 | tf_op jit(solution)/shard_map/while/body/eval_jaxpr/fdr,fre->fde/dot_general | solution.py:35
  20.2 0.6 dynamic_slice.25
  21.5 4.8 %fusion.55 = f32[1,64,10240]{2,1,0:T(8,128)S(1)} fusion(s32[10240]{0:T(1024)S(1)} %bitcast.87, s32[512]{0:T(512)S(1)} %bitcast.85, f32[1,64,10240]{2,1,0:T(8,128)S(1)} %get-tuple-element.264, pred[]{:T(512)S(6)} %compare.3, bf16[1,64,4096]{2,1,0:T(8,128)(2,1)} %get-tuple-element.275, s32[]{:T(128)S(6)} %select_n.63), kind=kOutput, calls=%fused_computation.5.clone.1 | convolution fusion | flops 677642240 | bytes 5351429 | tf_op jit(solution)/shard_map/while/body/eval_jaxpr/fdr,fre->fde/dot_general | solution.py:35
  26.3 0.6 dynamic_slice.25
  27.5 4.8 %fusion.55 = f32[1,64,10240]{2,1,0:T(8,128)S(1)} fusion(s32[10240]{0:T(1024)S(1)} %bitcast.87, s32[512]{0:T(512)S(1)} %bitcast.85, f32[1,64,10240]{2,1,0:T(8,128)S(1)} %get-tuple-element.264, pred[]{:T(512)S(6)} %compare.3, bf16[1,64,4096]{2,1,0:T(8,128)(2,1)} %get-tuple-element.275, s32[]{:T(128)S(6)} %select_n.63), kind=kOutput, calls=%fused_computation.5.clone.1 | convolution fusion | flops 677642240 | bytes 5351429 | tf_op jit(solution)/shard_map/while/body/eval_jaxpr/fdr,fre->fde/dot_general | solution.py:35
  32.4 0.6 dynamic_slice.25
  33.6 4.8 %fusion.55 = f32[1,64,10240]{2,1,0:T(8,128)S(1)} fusion(s32[10240]{0:T(1024)S(1)} %bitcast.87, s32[512]{0:T(512)S(1)} %bitcast.85, f32[1,64,10240]{2,1,0:T(8,128)S(1)} %get-tuple-element.264, pred[]{:T(512)S(6)} %compare.3, bf16[1,64,4096]{2,1,0:T(8,128)(2,1)} %get-tuple-element.275, s32[]{:T(128)S(6)} %select_n.63), kind=kOutput, calls=%fused_computation.5.clone.1 | convolution fusion | flops 677642240 | bytes 5351429 | tf_op jit(solution)/shard_map/while/body/eval_jaxpr/fdr,fre->fde/dot_general | solution.py:35
  38.4 0.6 dynamic_slice.25
  39.7 4.8 %fusion.55 = f32[1,64,10240]{2,1,0:T(8,128)S(1)} fusion(s32[10240]{0:T(1024)S(1)} %bitcast.87, s32[512]{0:T(512)S(1)} %bitcast.85, f32[1,64,10240]{2,1,0:T(8,128)S(1)} %get-tuple-element.264, pred[]{:T(512)S(6)} %compare.3, bf16[1,64,4096]{2,1,0:T(8,128)(2,1)} %get-tuple-element.275, s32[]{:T(128)S(6)} %select_n.63), kind=kOutput, calls=%fused_computation.5.clone.1 | convolution fusion | flops 677642240 | bytes 5351429 | tf_op jit(solution)/shard_map/while/body/eval_jaxpr/fdr,fre->fde/dot_general | solution.py:35
  44.5 0.6 dynamic_slice.25
  45.8 4.8 %fusion.55 = f32[1,64,10240]{2,1,0:T(8,128)S(1)} fusion(s32[10240]{0:T(1024)S(1)} %bitcast.87, s32[512]{0:T(512)S(1)} %bitcast.85, f32[1,64,10240]{2,1,0:T(8,128)S(1)} %get-tuple-element.264, pred[]{:T(512)S(6)} %compare.3, bf16[1,64,4096]{2,1,0:T(8,128)(2,1)} %get-tuple-element.275, s32[]{:T(128)S(6)} %select_n.63), kind=kOutput, calls=%fused_computation.5.clone.1 | convolution fusion | flops 677642240 | bytes 5351429 | tf_op jit(solution)/shard_map/while/body/eval_jaxpr/fdr,fre->fde/dot_general | solution.py:35
  50.6 0.6 dynamic_slice.25
  51.8 4.8 %fusion.55 = f32[1,64,10240]{2,1,0:T(8,128)S(1)} fusion(s32[10240]{0:T(1024)S(1)} %bitcast.87, s32[512]{0:T(512)S(1)} %bitcast.85, f32[1,64,10240]{2,1,0:T(8,128)S(1)} %get-tuple-element.264, pred[]{:T(512)S(6)} %compare.3, bf16[1,64,4096]{2,1,0:T(8,128)(2,1)} %get-tuple-element.275, s32[]{:T(128)S(6)} %select_n.63), kind=kOutput, calls=%fused_computation.5.clone.1 | convolution fusion | flops 677642240 | bytes 5351429 | tf_op jit(solution)/shard_map/while/body/eval_jaxpr/fdr,fre->fde/dot_general | solution.py:35
  56.6 0.0 copy-start.1
  56.6 0.0 copy-start.4
  56.7 0.0 copy-start.5
  56.7 0.1 convert_element_type.41
  56.8 0.2 copy.22
  57.0 0.4 copy-done.1
  57.4 0.1 bitcast_select_fusion
  57.5 5.2 %fusion.39 = f32[8,1,64,128]{3,2,0,1:T(8,128)} fusion(s32[8,1280]{1,0:T(8,128)S(1)} %bitcast_select_fusion, s32[8,1280]{1,0:T(8,128)S(1)} %bitcast.91, bf16[64,8,1280]{2,1,0:T(8,128)(2,1)S(1)} %bitcast.80), kind=kOutput, calls=%fused_computation.34 | convolution fusion | flops 171704320 | bytes 1654784 | tf_op jit(solution)/shard_map/fdnk,fnkj->nfdj/dot_general | solution.py:50
  62.6 0.0 reduce-scatter.2.cloned.1.call-update
  62.8 0.1 lt.56
  62.9 28.1 %all_gather.9 = bf16[1,64,1024]{2,1,0:T(8,128)(2,1)S(1)} all-gather(bf16[1,64,128]{2,1,0:T(8,128)(2,1)S(1)} %copy-done.2), channel_id=1, replica_groups=mesh['rows'=8,'dims'=4] {'rows'}, dimensions={2}, use_global_device_ids=true | all-gather | bytes 147456 | tf_op jit(solution)/shard_map/all_gather | solution.py:55
  91.0 3.1 %fusion.32 = bf16[1,8,8,8,1280]{4,3,2,1,0:T(8,128)(2,1)S(1)} fusion(s32[8,1280]{1,0:T(8,128)S(1)} %bitcast.92, bf16[64,8,128]{2,1,0:T(8,128)(2,1)S(1)} %bitcast.82), kind=kOutput, calls=%fused_computation.27 | convolution fusion | flops 169738240 | bytes 1482752 | tf_op jit(solution)/shard_map/fdnj,fnkj->fdnk/dot_general | solution.py:58
  94.2 0.1 copy.20
  94.3 0.1 fusion.43
  94.3 38.5 %while.24 = (s32[]{:T(128)}, f32[8,1,64,512]{3,2,1,0:T(8,128)S(1)}, s32[1,1,10240]{2,1,0:T(1,128)S(1)}, s32[8]{0:T(128)S(1)}, bf16[1,1,10240]{2,1,0:T(2,128)(2,1...) while((s32[]{:T(128)}, f32[8,1,64,512]{3,2,1,0:T(8,128)S(1)}, ...), condition=%wide.region_4.5_spmd.clone, body=%wide.region_3.4_spmd.clone.sunk | while | flops 681574912 | bytes 1548423 | solution.py:68
  94.4 0.6 dynamic_slice.23
  95.6 0.1 reduce.6
  95.7 3.4 %fusion.52 = f32[8,1,64,512]{3,2,1,0:T(8,128)S(1)} fusion(f32[8,1,64,512]{3,2,1,0:T(8,128)S(1)} %get-tuple-element.291, s32[]{:T(128)S(6)} %copy.39, bf16[1,64,10240]{2,1,0:T(8,128)(2,1)S(1)} %get-tuple-element.304, s32[10240]{0:T(1024)S(1)} %bitcast.88, s32[512]{0:T(512)S(1)} %bitcast.86, bf16[10240]{0:T(1024)(128)(2,1)S(1)} %reduce.6), kind=kOutput, calls=%fused_computation.20.clone.1 | convolution fusion | flops 681574400 | bytes 1505284 | tf_op jit(solution)/shard_map/while/body/eval_jaxpr/fde,fre->fdr/dot_general | solution.py:66
  99.2 0.6 dynamic_slice.23
  100.4 0.1 reduce.6
  100.5 3.4 %fusion.52 = f32[8,1,64,512]{3,2,1,0:T(8,128)S(1)} fusion(f32[8,1,64,512]{3,2,1,0:T(8,128)S(1)} %get-tuple-element.291, s32[]{:T(128)S(6)} %copy.39, bf16[1,64,10240]{2,1,0:T(8,128)(2,1)S(1)} %get-tuple-element.304, s32[10240]{0:T(1024)S(1)} %bitcast.88, s32[512]{0:T(512)S(1)} %bitcast.86, bf16[10240]{0:T(1024)(128)(2,1)S(1)} %reduce.6), kind=kOutput, calls=%fused_computation.20.clone.1 | convolution fusion | flops 681574400 | bytes 1505284 | tf_op jit(solution)/shard_map/while/body/eval_jaxpr/fde,fre->fdr/dot_general | solution.py:66
  104.0 0.6 dynamic_slice.23
  105.2 0.1 reduce.6
  105.3 3.4 %fusion.52 = f32[8,1,64,512]{3,2,1,0:T(8,128)S(1)} fusion(f32[8,1,64,512]{3,2,1,0:T(8,128)S(1)} %get-tuple-element.291, s32[]{:T(128)S(6)} %copy.39, bf16[1,64,10240]{2,1,0:T(8,128)(2,1)S(1)} %get-tuple-element.304, s32[10240]{0:T(1024)S(1)} %bitcast.88, s32[512]{0:T(512)S(1)} %bitcast.86, bf16[10240]{0:T(1024)(128)(2,1)S(1)} %reduce.6), kind=kOutput, calls=%fused_computation.20.clone.1 | convolution fusion | flops 681574400 | bytes 1505284 | tf_op jit(solution)/shard_map/while/body/eval_jaxpr/fde,fre->fdr/dot_general | solution.py:66
  108.8 0.6 dynamic_slice.23
  110.0 0.1 reduce.6
  110.1 3.4 %fusion.52 = f32[8,1,64,512]{3,2,1,0:T(8,128)S(1)} fusion(f32[8,1,64,512]{3,2,1,0:T(8,128)S(1)} %get-tuple-element.291, s32[]{:T(128)S(6)} %copy.39, bf16[1,64,10240]{2,1,0:T(8,128)(2,1)S(1)} %get-tuple-element.304, s32[10240]{0:T(1024)S(1)} %bitcast.88, s32[512]{0:T(512)S(1)} %bitcast.86, bf16[10240]{0:T(1024)(128)(2,1)S(1)} %reduce.6), kind=kOutput, calls=%fused_computation.20.clone.1 | convolution fusion | flops 681574400 | bytes 1505284 | tf_op jit(solution)/shard_map/while/body/eval_jaxpr/fde,fre->fdr/dot_general | solution.py:66
  113.6 0.6 dynamic_slice.23
  114.8 0.1 reduce.6
  115.0 3.4 %fusion.52 = f32[8,1,64,512]{3,2,1,0:T(8,128)S(1)} fusion(f32[8,1,64,512]{3,2,1,0:T(8,128)S(1)} %get-tuple-element.291, s32[]{:T(128)S(6)} %copy.39, bf16[1,64,10240]{2,1,0:T(8,128)(2,1)S(1)} %get-tuple-element.304, s32[10240]{0:T(1024)S(1)} %bitcast.88, s32[512]{0:T(512)S(1)} %bitcast.86, bf16[10240]{0:T(1024)(128)(2,1)S(1)} %reduce.6), kind=kOutput, calls=%fused_computation.20.clone.1 | convolution fusion | flops 681574400 | bytes 1505284 | tf_op jit(solution)/shard_map/while/body/eval_jaxpr/fde,fre->fdr/dot_general | solution.py:66
  118.4 0.6 dynamic_slice.23
  119.7 0.1 reduce.6
  119.8 3.4 %fusion.52 = f32[8,1,64,512]{3,2,1,0:T(8,128)S(1)} fusion(f32[8,1,64,512]{3,2,1,0:T(8,128)S(1)} %get-tuple-element.291, s32[]{:T(128)S(6)} %copy.39, bf16[1,64,10240]{2,1,0:T(8,128)(2,1)S(1)} %get-tuple-element.304, s32[10240]{0:T(1024)S(1)} %bitcast.88, s32[512]{0:T(512)S(1)} %bitcast.86, bf16[10240]{0:T(1024)(128)(2,1)S(1)} %reduce.6), kind=kOutput, calls=%fused_computation.20.clone.1 | convolution fusion | flops 681574400 | bytes 1505284 | tf_op jit(solution)/shard_map/while/body/eval_jaxpr/fde,fre->fdr/dot_general | solution.py:66
  123.2 0.6 dynamic_slice.23
  124.5 0.1 reduce.6
  124.6 3.4 %fusion.52 = f32[8,1,64,512]{3,2,1,0:T(8,128)S(1)} fusion(f32[8,1,64,512]{3,2,1,0:T(8,128)S(1)} %get-tuple-element.291, s32[]{:T(128)S(6)} %copy.39, bf16[1,64,10240]{2,1,0:T(8,128)(2,1)S(1)} %get-tuple-element.304, s32[10240]{0:T(1024)S(1)} %bitcast.88, s32[512]{0:T(512)S(1)} %bitcast.86, bf16[10240]{0:T(1024)(128)(2,1)S(1)} %reduce.6), kind=kOutput, calls=%fused_computation.20.clone.1 | convolution fusion | flops 681574400 | bytes 1505284 | tf_op jit(solution)/shard_map/while/body/eval_jaxpr/fde,fre->fdr/dot_general | solution.py:66
  128.0 0.6 dynamic_slice.23
  129.3 0.1 reduce.6
  129.4 3.4 %fusion.52 = f32[8,1,64,512]{3,2,1,0:T(8,128)S(1)} fusion(f32[8,1,64,512]{3,2,1,0:T(8,128)S(1)} %get-tuple-element.291, s32[]{:T(128)S(6)} %copy.39, bf16[1,64,10240]{2,1,0:T(8,128)(2,1)S(1)} %get-tuple-element.304, s32[10240]{0:T(1024)S(1)} %bitcast.88, s32[512]{0:T(512)S(1)} %bitcast.86, bf16[10240]{0:T(1024)(128)(2,1)S(1)} %reduce.6), kind=kOutput, calls=%fused_computation.20.clone.1 | convolution fusion | flops 681574400 | bytes 1505284 | tf_op jit(solution)/shard_map/while/body/eval_jaxpr/fde,fre->fdr/dot_general | solution.py:66
  132.8 0.2 multiply_reduce_fusion
  133.0 0.1 copy.21
  133.1 5.2 %all_gather.11 = f32[4,1,4096]{2,1,0:T(1,128)S(1)} all-gather(f32[1,1,4096]{2,1,0:T(1,128)S(1)} %all_gather.10), channel_id=1, replica_groups=mesh['rows'=8,'dims'=4] {'dims'}, dimensions={0}, use_global_device_ids=true | all-gather | bytes 81920 | tf_op jit(solution)/shard_map/all_gather | solution.py:71
  138.4 0.1 reduce_sum.19
  138.5 0.6 fusion.45
  139.1 0.9 subtract_convert_fusion
  (36 shorter events, 0.3 us)
Async XLA Ops:
  7.2 132.9 %reduce-scatter.2.cloned.1.call-start = ((), (), s32[]{:S(2)}) async-start(), calls=%async_computation.1 | async-start | bytes 294912 | tf_op jit(solution)/shard_map/reduce_scatter | solution.py:49
  56.6 0.8 copy-start.1
  56.6 0.8 copy-start.4
  56.7 0.8 copy-start.5
  57.5 5.4 %copy-start.2 = (bf16[1,64,128]{2,1,0:T(8,128)(2,1)S(1)}, bf16[1,64,128]{2,1,0:T(8,128)(2,1)}, u32[]{:S(2)}) copy-start(bf16[1,64,128]{2,1,0:T(8,128)(2,1)} %param.13) | copy-start | bytes 49156
  132.8 5.6 %copy-start.3 = (f32[1,4096]{1,0:T(1,128)S(1)}, f32[1,4096]{1,0:T(1,128)}, u32[]{:S(2)}) copy-start(f32[1,4096]{1,0:T(1,128)} %param.12) | copy-start | bytes 49156
  132.8 6.3 %copy-start = (bf16[1,64,4096]{2,1,0:T(8,128)(2,1)S(1)}, bf16[1,64,4096]{2,1,0:T(8,128)(2,1)}, u32[]{:S(2)}) copy-start(bf16[1,64,4096]{2,1,0:T(8,128)(2,1)} %get-tuple-element.309) | copy-start | bytes 1572868
Sparse Core Ops, SparseCore 0:
  62.8 64.8 reduce-scatter.1
